TPU v7x, 32 devices: a whole 2x2x4 slice. The times are simulated.
32 devices in a mesh: dp: 4 (over x, core), tensor: 8 (over z, y).
Axes of the slice: x: 2, y: 2, z: 4, core: 2. Of those that a mesh axis runs over, the one named last changes fastest.
Arguments:
- queries: bfloat16 [2048, 8192], P('dp', 'tensor'), may hold values from -60 to 60
- keys_values: bfloat16 [2, 2048, 1024], P(None, 'dp'), may hold values from -7 to 7
- out_weight: bfloat16 [8192, 8192], P('tensor'), may hold values from -0.0625 to 0.0625
- cotangent: bfloat16 [2048, 8192], P(('dp', 'tensor')), may hold values from -6 to 6
- head_pick: int32 [12, 64], replicated, may hold values from 0 to 1, as said below
- owner_index: int32 [12, 1], replicated, may hold values from 0 to 3; in each aligned block of 12 rows (0 to 11, 12 to 23, ...) at most 3 rows name the same one
Outputs:
- query_grad: bfloat16 [2048, 8192], P('dp', 'tensor')
- weight_grad: float32 [12, 128, 8192], P('dp', None, 'tensor')
Inputs may be any that keep to these rules, and one draw needn't show every extreme that they name: `head_pick`: each row has a single 1; no head is named twice. `owner_index`: no data index owns more than 3 selected heads, and one owns exactly 3.
All inputs are finite; a program needn't handle non-finite values.
Results may differ from a plain program's by a relative error of at most 0.008.
Values may be sent and summed in bfloat16 or wider, within the bound.
A program may use at most 192 MiB of HBM per device.

v0:
```python
import math

import jax
import jax.numpy as jnp
from jax import lax
from jax.sharding import PartitionSpec as P

H = 64
HD = 128
KVH = 8
CAP = 3


def route_table(owner_index, groups, capacity):
    chosen = owner_index[:, 0]
    picked_count = chosen.shape[0]
    matches = (chosen[:, None] == chosen[None, :]).astype(jnp.int32)
    order = jnp.arange(picked_count, dtype=jnp.int32)
    earlier = (order[:, None] > order[None, :]).astype(jnp.int32)
    slot_index = jnp.sum(matches * earlier, axis=1)
    target = chosen * capacity + slot_index
    places = jnp.arange(groups * capacity, dtype=jnp.int32)
    return (places[:, None] == target[None, :]).astype(jnp.float32)


def column_product(picked, full_grad, column_start, column_width):
    column_slab = lax.dynamic_slice_in_dim(full_grad, column_start, column_width, 1)
    return jnp.einsum("tsd,tc->sdc", picked, column_slab, preferred_element_type=jnp.float32)


def on_device(queries, keys_values, out_weight, cotangent, head_pick, owner_index):
    tensor_size = lax.axis_size("tensor")
    tensor_rank = lax.axis_index("tensor")
    group_rows = queries.shape[0]
    local_heads = queries.shape[1] // HD
    kv_head = tensor_rank * local_heads // (H // KVH)
    kv_local = lax.dynamic_slice_in_dim(keys_values, kv_head * HD, HD, 2)
    key_block = kv_local[0]
    value_block = kv_local[1]
    full_grad = lax.all_gather(cotangent, "tensor", axis=0, tiled=True)
    score_scale = 1.0 / math.sqrt(HD)
    query_heads = queries.reshape(group_rows, local_heads, HD)
    scores = (
        jnp.einsum("thd,sd->hts", query_heads, key_block, preferred_element_type=jnp.float32)
        * score_scale
    )
    positions = jnp.arange(group_rows, dtype=jnp.int32)
    allowed = positions[:, None] >= positions[None, :]
    scores = jnp.where(allowed[None], scores, -jnp.inf)
    peak = jnp.max(scores, axis=2, keepdims=True)
    weights = jnp.exp(scores - peak)
    probs = weights / jnp.sum(weights, axis=2, keepdims=True)
    attended = jnp.einsum(
        "hts,sd->thd", probs.astype(jnp.bfloat16), value_block, preferred_element_type=jnp.float32
    ).astype(jnp.bfloat16)
    input_grad = lax.dot_general(
        full_grad, out_weight, (((1,), (1,)), ((), ())), preferred_element_type=jnp.float32
    )
    input_grad = input_grad.astype(jnp.bfloat16).reshape(group_rows, local_heads, HD)
    prob_grad = jnp.einsum(
        "thd,sd->hts", input_grad, value_block, preferred_element_type=jnp.float32
    )
    row_delta = jnp.transpose(
        jnp.sum(input_grad.astype(jnp.float32) * attended.astype(jnp.float32), axis=2)
    )
    score_grad = (probs * (prob_grad - row_delta[:, :, None])).astype(jnp.bfloat16)
    query_grad = (
        jnp.einsum("hts,sd->thd", score_grad, key_block, preferred_element_type=jnp.float32)
        * score_scale
    )
    query_grad = query_grad.astype(jnp.bfloat16).reshape(group_rows, local_heads * HD)
    column_width = full_grad.shape[1] // tensor_size
    column_start = tensor_rank * column_width
    whole_attended = lax.all_gather(
        attended.reshape(group_rows, local_heads * HD), "tensor", axis=1, tiled=True
    )
    picked = jnp.einsum(
        "sh,thd->tsd",
        head_pick.astype(jnp.bfloat16),
        whole_attended.reshape(group_rows, -1, HD),
        preferred_element_type=jnp.float32,
    ).astype(jnp.bfloat16)
    selected = column_product(picked, full_grad, column_start, column_width)
    routing = route_table(owner_index, lax.axis_size("dp"), CAP)
    sectioning = jnp.einsum("ps,sdc->pdc", routing, selected, precision=lax.Precision.HIGHEST)
    owned = lax.psum_scatter(sectioning, "dp", scatter_dimension=0, tiled=True)
    return (query_grad, owned)


def solution(mesh):
    placed = (
        P("dp", "tensor"),
        P(None, "dp", None),
        P("tensor", None),
        P(("dp", "tensor"), None),
        P(),
        P(),
    )
    return jax.shard_map(
        on_device,
        mesh=mesh,
        in_specs=placed,
        out_specs=(P("dp", "tensor"), P("dp", None, "tensor")),
        check_vma=False,
    )
```

profile of v0, /device:TPU:0, one launch (start us, length us, event | category | flops | bytes accessed | tf_op | source)
XLA Modules:
  0.0 380.4 jit_solution(14811210492865165725)
XLA Ops:
  7.2 0.0 copy-start
  7.2 0.0 all-gather.3.cloned.1.call-start
  7.2 0.7 all-gather.3.cloned.1.call-update
  7.9 0.0 all-gather.5.cloned.1.call-start
  8.0 0.1 iota_compare_fusion
  8.1 0.7 copy-done
  8.8 2.5 fusion.23
  11.2 5.6 %fusion.40 = (f32[8,512]{1,0:T(8,128)S(1)}, f32[8,512,512]{1,2,0:T(8,128)}) fusion(f32[512,512,8]{1,0,2:T(8,128)S(1)} %fusion.23, pred[512,512]{0,1:T(8,128)(4,1)S(1)} %iota_compare_fusion), kind=kOutput, calls=%fused_computation.47 | output fusion | flops 12583423 | bytes 17055744 | tf_op jit(solution)/shard_map/sub | solution.py:51
  16.8 120.5 %all-gather.3.cloned.1.call-done = bf16[512,8192]{1,0:T(8,128)(2,1)} async-done(((bf16[64,8192]{1,0:T(8,128)(2,1)}), bf16[512,8192]{1,0:T(8,128)(2,1)}) %all-gather.3.cloned.1.call-update) | async-done | bytes 8388624 | tf_op jit(solution)/shard_map/all_gather | solution.py:40
  137.3 15.6 %convolution_convert_fusion = bf16[512,1024]{1,0:T(8,128)(2,1)} fusion(bf16[512,8192]{1,0:T(8,128)(2,1)} %all-gather.3.cloned.1.call-done, bf16[1024,8192]{1,0:T(8,128)(2,1)} %param.8), kind=kOutput, calls=%fused_computation.24 | convolution fusion | flops 8590458880 | bytes 26214400 | tf_op jit(solution)/shard_map/dot_general | solution.py:56
  153.0 1.5 copy.43
  154.5 0.0 copy-start.2
  154.5 5.5 %multiply_reduce_fusion = (f32[512,8]{0,1:T(8,128)S(1)}, bf16[128,8,512]{2,0,1:T(8,128)(2,1)}) fusion(bf16[512,1024]{0,1:T(8,128)(2,1)S(1)} %copy.43, f32[8,512,512]{1,2,0:T(8,128)} %get-tuple-element.9, f32[8,512]{1,0:T(8,128)S(1)} %get-tuple-element.8, bf16[2,512,1024]{2,1,0:T(8,128)(2,1)S(1)} %copy-done, s32[]{:T(128)S(6)} %add.19, s32[]{:T(128)S(6)} %select_n.16), kind=kOutput, calls=%fused_computation.20 | convolution fusion | flops 543682560 | bytes 10649608 | tf_op jit(solution)/shard_map/hts,sd->thd/dot_general | solution.py:53
  159.9 0.0 all-gather.5.cloned.1.call-update
  159.9 0.0 reduce-scatter.2.cloned.1.call-start
  160.0 0.0 copy-done.2
  160.0 0.2 select_reduce_fusion
  160.2 122.6 %all-gather.5.cloned.1.call-done = bf16[512,8192]{0,1:T(8,128)(2,1)} async-done(((bf16[512,1024]{0,1:T(8,128)(2,1)}), bf16[512,8192]{0,1:T(8,128)(2,1)}) %all-gather.5.cloned.1.call-update) | async-done | bytes 8388624 | tf_op jit(solution)/shard_map/all_gather | solution.py:74
  282.8 0.0 copy-start.1
  282.8 12.1 %copy.42 = bf16[512,64,128]{2,1,0:T(8,128)(2,1)} copy(bf16[512,64,128]{0,2,1:T(8,128)(2,1)} %bitcast.72) | data formatting | bytes 16777216 | tf_op jit(solution)/shard_map/reshape | solution.py:80
  294.8 0.0 copy-done.1
  294.8 4.6 %convert_bitcast_fusion = bf16[512,12,128]{2,1,0:T(8,128)(2,1)S(1)} fusion(bf16[512,64,128]{2,1,0:T(8,128)(2,1)} %copy.42, s32[12,64]{1,0:T(8,128)S(1)} %copy-done.1), kind=kOutput, calls=%fused_computation.18 | convolution fusion | flops 101450496 | bytes 9964544 | tf_op jit(solution)/shard_map/sh,thd->tsd/dot_general | solution.py:77
  299.4 3.1 fusion.16
  302.5 7.5 %fusion.3 = f32[12,128,1024]{2,0,1:T(8,128)S(1)} fusion(f32[12,128,1024]{2,1,0:T(8,128)S(1)} %fusion.16, s32[12]{0:T(128)S(1)} %multiply_add_fusion), kind=kOutput, calls=%fused_computation.5 | convolution fusion | flops 226492560 | bytes 12582960 | tf_op jit(solution)/shard_map/ps,sdc->pdc/dot_general | solution.py:85
  310.0 6.6 %copy.34 = f32[12,128,1024]{2,1,0:T(8,128)} copy(f32[12,128,1024]{2,0,1:T(8,128)S(1)} %fusion.3) | data formatting | bytes 12582912 | tf_op jit(solution)/shard_map/ps,sdc->pdc/dot_general | solution.py:85
  316.6 0.0 reduce-scatter.2.cloned.1.call-update
  316.6 6.2 %multiply_convert_fusion = bf16[128,8,512]{2,0,1:T(8,128)(2,1)} fusion(f32[8,512]{1,0:T(8,128)S(1)} %bitcast.77, bf16[512,8,128]{0,2,1:T(8,128)(2,1)S(1)} %bitcast.73, f32[8,512,512]{1,2,0:T(8,128)} %get-tuple-element.9, f32[8,512]{1,0:T(8,128)S(1)} %get-tuple-element.8, bf16[2,512,1024]{2,1,0:T(8,128)(2,1)S(1)} %copy-done, s32[]{:T(128)S(6)} %select_n.16, ...), kind=kOutput, calls=%fused_computation.19 | convolution fusion | flops 1083179008 | bytes 10782208 | tf_op jit(solution)/shard_map/hts,sd->thd/dot_general | solution.py:68
  322.9 2.6 copy.35
  325.4 48.4 %reduce-scatter.2.cloned.1.call-done = f32[3,128,1024]{2,1,0:T(8,128)} async-done(((f32[12,128,1024]{2,1,0:T(8,128)}), f32[3,128,1024]{2,1,0:T(8,128)}) %reduce-scatter.2.cloned.1.call-update) | async-done | bytes 1572880 | tf_op jit(solution)/shard_map/reduce_scatter | solution.py:86
  (1 shorter events, 0.0 us)
Async XLA Ops:
  7.2 1.6 copy-start
  7.2 130.2 %all-gather.3.cloned.1.call-start = ((), (), s32[]{:S(2)}) async-start(), calls=%async_computation.1 | async-start | bytes 9437184 | tf_op jit(solution)/shard_map/all_gather | solution.py:40
  7.9 274.9 %all-gather.5.cloned.1.call-start = ((), (), s32[]{:S(2)}) async-start(), calls=%async_computation.2 | async-start | bytes 9437184 | tf_op jit(solution)/shard_map/all_gather | solution.py:74
  154.5 5.5 %copy-start.2 = (s32[12,1]{0,1:T(1,128)S(1)}, s32[12,1]{0,1:T(1,128)}, u32[]{:S(2)}) copy-start(s32[12,1]{0,1:T(1,128)} %param.11) | copy-start | bytes 148
  159.9 213.9 %reduce-scatter.2.cloned.1.call-start = ((), (), s32[]{:S(2)}) async-start(), calls=%async_computation.3 | async-start | bytes 7864320 | tf_op jit(solution)/shard_map/reduce_scatter | solution.py:86
  282.8 12.1 %copy-start.1 = (s32[12,64]{1,0:T(8,128)S(1)}, s32[12,64]{1,0:T(8,128)}, u32[]{:S(2)}) copy-start(s32[12,64]{1,0:T(8,128)} %param.10) | copy-start | bytes 9220
Sparse Core Ops, SparseCore 0:
  10.1 127.1 all-gather.2
  160.1 122.6 all-gather.4
  316.8 57.0 reduce-scatter.1
where the time goes:
time: 381 us; the launch traced here: 380 us
  waiting for transfers between devices  292 us (77%)
  matrix products  45 us (12%)
  local copies, waits for them, and re-layouts  23.4 us (6%)
  between operations  13.8 us (4%)
  other arithmetic  5.83 us (2%)
    all_gather x1, waiting for transfers between devices, on_device(): lax.all_gather(attended.reshape(group_rows, local_heads * HD), 'tensor',...  123 us
    all_gather x1, waiting for transfers between devices, on_device(): full_grad = lax.all_gather(cotangent, 'tensor', axis=0, tiled=True)  121 us
    reduce_scatter x1, waiting for transfers between devices, on_device(): owned = lax.psum_scatter(sectioning, 'dp', scatter_dimension=0, tiled=True)  48.4 us
    dot_general x1, matrix products, on_device(): lax.dot_general(full_grad, out_weight, (((1,), (1,)), ((), ())), preferre...  15.6 us
    reshape x1, local copies, waits for them, and re-layouts, on_device(): whole_attended.reshape(group_rows, -1, HD)  12.1 us
  transfers between devices with their start and end apart: 3, of which 3 were waited for; matrix products, arithmetic and copies ran while one was open for 4% of the time, Pallas kernels for 0%

commit v1 on v0

--- a/solution.py
+++ b/solution.py
@@ -1,14 +1,18 @@
+import functools
 import math
 
 import jax
 import jax.numpy as jnp
 from jax import lax
+from jax.experimental import pallas as pl
+from jax.experimental.pallas import tpu as pltpu
 from jax.sharding import PartitionSpec as P
 
 H = 64
 HD = 128
 KVH = 8
 CAP = 3
+MESH = pl.DeviceIdType.MESH
 
 
 def route_table(owner_index, groups, capacity):
@@ -23,9 +27,139 @@
     return (places[:, None] == target[None, :]).astype(jnp.float32)
 
 
-def column_product(picked, full_grad, column_start, column_width):
-    column_slab = lax.dynamic_slice_in_dim(full_grad, column_start, column_width, 1)
-    return jnp.einsum("tsd,tc->sdc", picked, column_slab, preferred_element_type=jnp.float32)
+def ring_member(place, n):
+    late = place // (n // 2)
+    return (1 - late) * (2 * place) + late * (2 * (n - 1 - place) + 1)
+
+
+def ring_place(index, n):
+    odd = index % 2
+    return (1 - odd) * (index // 2) + odd * (n - 1 - index // 2)
+
+
+def slot_of(direction, hop, n):
+    if hop == 0:
+        return 0
+    if hop == n // 2:
+        return n - 1
+    return 2 * hop - 1 + direction
+
+
+def gather_kernel(n, cot_ref, w_ref, ig_ref, slab_ref, held, wbuf, acc, send_sem, recv_sem, local_sem):
+    rows, width = cot_ref.shape
+    half = width // 2
+    last = n // 2
+    me = lax.axis_index("tensor")
+    place = ring_place(me, n)
+    to = (ring_member((place + 1) % n, n), ring_member((place + n - 1) % n, n))
+
+    w_copy = pltpu.make_async_copy(w_ref, wbuf, local_sem.at[0])
+    w_copy.start()
+    own_copy = pltpu.make_async_copy(cot_ref, held.at[0], local_sem.at[1])
+    own_copy.start()
+
+    barrier = pltpu.get_barrier_semaphore()
+    for target in to:
+        pl.semaphore_signal(barrier, inc=1, device_id={"tensor": target}, device_id_type=MESH)
+    pl.semaphore_wait(barrier, 2)
+
+    def send(direction, hop, part):
+        columns = pl.ds(part * half, half)
+        source = cot_ref if hop == 1 else held.at[slot_of(direction, hop - 1, n)]
+        return pltpu.make_async_remote_copy(
+            src_ref=source.at[:, columns],
+            dst_ref=held.at[slot_of(direction, hop, n), :, columns],
+            send_sem=send_sem.at[direction, hop - 1, part],
+            recv_sem=recv_sem.at[direction, hop - 1, part],
+            device_id={"tensor": to[direction]},
+            device_id_type=MESH,
+        )
+
+    def parts(direction, hop):
+        order = (0, 1) if direction == 0 else (1, 0)
+        return order if hop < last else order[:1]
+
+    sent = {}
+    for turn in range(2):
+        for direction in range(2):
+            part = parts(direction, 1)[turn]
+            sent[direction, 1, part] = send(direction, 1, part)
+            sent[direction, 1, part].start()
+
+    own_copy.wait()
+    w_copy.wait()
+    step = 1024
+    my_columns = pl.ds(pl.multiple_of(me * (width // n), width // n), width // n)
+
+    def product(first, count):
+        acc[...] = jnp.zeros_like(acc)
+
+        def body(k, carry):
+            columns = pl.ds(pl.multiple_of(k * step, step), step)
+            block = held[first : first + count, :, columns].reshape(count * rows, step)
+            acc[: count * rows, :] += lax.dot_general(
+                block,
+                wbuf[:, columns],
+                (((1,), (1,)), ((), ())),
+                preferred_element_type=jnp.float32,
+            )
+            return carry
+
+        lax.fori_loop(0, width // step, body, 0)
+
+    def store(slot, at, origin):
+        target = pl.ds(pl.multiple_of(origin * rows, rows), rows)
+        ig_ref[target, :] = acc[at * rows : (at + 1) * rows, :].astype(ig_ref.dtype)
+        slab_ref[target, :] = held[slot, :, my_columns]
+
+    product(0, 1)
+    store(0, 0, me)
+    for hop in range(1, last + 1):
+        turns = 2 if hop < last else 1
+        for turn in range(turns):
+            for direction in range(2):
+                part = parts(direction, hop)[turn]
+                sent[direction, hop, part].wait_recv()
+                if hop < last and part in parts(direction, hop + 1):
+                    sent[direction, hop + 1, part] = send(direction, hop + 1, part)
+                    sent[direction, hop + 1, part].start()
+        first = slot_of(0, hop, n)
+        product(first, turns)
+        for direction in range(turns):
+            shift = n - hop if direction == 0 else hop
+            store(first + direction, direction, ring_member((place + shift) % n, n))
+    for copy in sent.values():
+        copy.wait_send()
+
+
+def gather_and_multiply(cotangent, out_weight, n):
+    rows, width = cotangent.shape
+    outs = out_weight.shape[0]
+    return pl.pallas_call(
+        functools.partial(gather_kernel, n),
+        out_shape=(
+            jax.ShapeDtypeStruct((n * rows, outs), jnp.bfloat16),
+            jax.ShapeDtypeStruct((n * rows, width // n), jnp.bfloat16),
+        ),
+        in_specs=[pl.BlockSpec(memory_space=pl.ANY)] * 2,
+        out_specs=(pl.BlockSpec(memory_space=pltpu.VMEM),) * 2,
+        scratch_shapes=[
+            pltpu.VMEM((n, rows, width), jnp.bfloat16),
+            pltpu.VMEM((outs, width), jnp.bfloat16),
+            pltpu.VMEM((2 * rows, outs), jnp.float32),
+            pltpu.SemaphoreType.DMA((2, n // 2, 2)),
+            pltpu.SemaphoreType.DMA((2, n // 2, 2)),
+            pltpu.SemaphoreType.DMA((2,)),
+        ],
+        compiler_params=pltpu.CompilerParams(
+            collective_id=0, has_side_effects=True, vmem_limit_bytes=48 * 1024 * 1024
+        ),
+        cost_estimate=pl.CostEstimate(
+            flops=2 * n * rows * width * outs,
+            bytes_accessed=2 * width * (outs + 16 * n * rows),
+            transcendentals=0,
+        ),
+    )(cotangent, out_weight)
 
 
 def on_device(queries, keys_values, out_weight, cotangent, head_pick, owner_index):
@@ -37,7 +171,6 @@
     kv_local = lax.dynamic_slice_in_dim(keys_values, kv_head * HD, HD, 2)
     key_block = kv_local[0]
     value_block = kv_local[1]
-    full_grad = lax.all_gather(cotangent, "tensor", axis=0, tiled=True)
     score_scale = 1.0 / math.sqrt(HD)
     query_heads = queries.reshape(group_rows, local_heads, HD)
     scores = (
@@ -53,10 +186,29 @@
     attended = jnp.einsum(
         "hts,sd->thd", probs.astype(jnp.bfloat16), value_block, preferred_element_type=jnp.float32
     ).astype(jnp.bfloat16)
-    input_grad = lax.dot_general(
-        full_grad, out_weight, (((1,), (1,)), ((), ())), preferred_element_type=jnp.float32
-    )
-    input_grad = input_grad.astype(jnp.bfloat16).reshape(group_rows, local_heads, HD)
+
+    routing = route_table(owner_index, lax.axis_size("dp"), CAP)
+    places = routing.shape[0]
+    local_pick = lax.dynamic_slice_in_dim(head_pick, tensor_rank * local_heads, local_heads, 1)
+    wanted = jnp.sum(routing[:, :, None] * local_pick.astype(jnp.float32)[None], axis=1)
+    chooser = (
+        wanted.T.astype(jnp.bfloat16)[:, None, :, None]
+        * jnp.eye(HD, dtype=jnp.bfloat16)[None, :, None, :]
+    ).reshape(local_heads * HD, places * HD)
+    mine = jnp.dot(
+        attended.reshape(group_rows, local_heads * HD), chooser, preferred_element_type=jnp.float32
+    ).astype(jnp.bfloat16)
+    picked = lax.psum(mine, "tensor")
+
+    input_grad, column_slab = gather_and_multiply(cotangent, out_weight, tensor_size)
+
+    selected = lax.dot_general(
+        picked, column_slab, (((0,), (0,)), ((), ())), preferred_element_type=jnp.float32
+    ).astype(jnp.bfloat16)
+    owned = lax.psum_scatter(selected, "dp", scatter_dimension=0, tiled=True)
+    owned = owned.astype(jnp.float32).reshape(CAP, HD, -1)
+
+    input_grad = input_grad.reshape(group_rows, local_heads, HD)
     prob_grad = jnp.einsum(
         "thd,sd->hts", input_grad, value_block, preferred_element_type=jnp.float32
     )
@@ -69,21 +221,6 @@
         * score_scale
     )
     query_grad = query_grad.astype(jnp.bfloat16).reshape(group_rows, local_heads * HD)
-    column_width = full_grad.shape[1] // tensor_size
-    column_start = tensor_rank * column_width
-    whole_attended = lax.all_gather(
-        attended.reshape(group_rows, local_heads * HD), "tensor", axis=1, tiled=True
-    )
-    picked = jnp.einsum(
-        "sh,thd->tsd",
-        head_pick.astype(jnp.bfloat16),
-        whole_attended.reshape(group_rows, -1, HD),
-        preferred_element_type=jnp.float32,
-    ).astype(jnp.bfloat16)
-    selected = column_product(picked, full_grad, column_start, column_width)
-    routing = route_table(owner_index, lax.axis_size("dp"), CAP)
-    sectioning = jnp.einsum("ps,sdc->pdc", routing, selected, precision=lax.Precision.HIGHEST)
-    owned = lax.psum_scatter(sectioning, "dp", scatter_dimension=0, tiled=True)
     return (query_grad, owned)
 
 

time: 381 us -> 260 us (0.68)
  waiting for transfers between devices: 292 us -> 117 us
  Pallas kernels: 0 us -> 90.2 us
  matrix products: 45 us -> 21.1 us
  local copies, waits for them, and re-layouts: 23.4 us -> 8.33 us
    all_gather x2 -> x0, waiting for transfers between devices: 243 us -> none  [the longest x1 123 us: on_device(): lax.all_gather(attended.reshape(group_rows, local_heads * HD), 'tensor',...]
    pallas_call x0 -> x1, Pallas kernels: none -> 90.2 us  [gather_and_multiply(): pl.pallas_call(functools.partial(gather_kernel, n), out_shape=(jax.ShapeD...]
    psum x0 -> x1, waiting for transfers between devices: none -> 89.3 us  [on_device(): picked = lax.psum(mine, 'tensor')]
    dot_general x4 -> x2, matrix products: 30.8 us -> 7.99 us  [the longest x1 5 us: on_device(): lax.dot_general(picked, column_slab, (((0,), (0,)), ((), ())), preferred_...]
    reduce_scatter x1, waiting for transfers between devices: 48.4 us -> 27.5 us  [on_device(): owned = lax.psum_scatter(selected, 'dp', scatter_dimension=0, tiled=True)]
    reshape x2 -> x1, local copies, waits for them, and re-layouts: 13.6 us -> 1.32 us  [on_device(): input_grad = input_grad.reshape(group_rows, local_heads, HD)]
    dot_general x1 -> x0, local copies, waits for them, and re-layouts: 6.58 us -> none  [on_device(): jnp.einsum('ps,sdc->pdc', routing, selected, precision=lax.Precision.HIGH...]
  transfers between devices with their start and end apart: 3 -> 2, of which waited for: 3 -> 2; matrix products, arithmetic and copies ran while one was open for 4% -> 3% of each run, Pallas kernels for 0% -> 0%
where the time goes in v1:
time: 260 us
  waiting for transfers between devices  117 us (45%)
  Pallas kernels  90.2 us (35%)
  matrix products  21.1 us (8%)
  between operations  14.2 us (5%)
  other arithmetic  8.69 us (3%)
  local copies, waits for them, and re-layouts  8.33 us (3%)
    pallas_call x1, Pallas kernels, gather_and_multiply(): pl.pallas_call(functools.partial(gather_kernel, n), out_shape=(jax.ShapeD...  90.2 us
    psum x1, waiting for transfers between devices, on_device(): picked = lax.psum(mine, 'tensor')  89.3 us
    reduce_scatter x1, waiting for transfers between devices, on_device(): owned = lax.psum_scatter(selected, 'dp', scatter_dimension=0, tiled=True)  27.5 us
    unnamed x18, local copies, waits for them, and re-layouts  6.94 us
    dot_general x1, matrix products, on_device(): jnp.einsum('hts,sd->thd', score_grad, key_block, preferred_element_type=j...  6.2 us
    sub x1, other arithmetic, on_device(): weights = jnp.exp(scores - peak)  5.56 us
  transfers between devices with their start and end apart: 2, of which 2 were waited for; matrix products, arithmetic and copies ran while one was open for 3% of the time, Pallas kernels for 0%

profile of v1, /device:TPU:0, one launch (start us, length us, event | category | flops | bytes accessed | tf_op | source)
XLA Modules:
  0.0 259.7 jit_solution(14017361869104030794)
XLA Ops:
  7.2 0.0 copy-start
  7.2 0.0 all-reduce.2.cloned.1.call-start
  7.2 0.1 iota_compare_fusion
  7.4 0.0 copy-start.1
  7.4 1.3 copy-done.1
  8.7 90.2 %shard_map.77 = (bf16[512,1024]{1,0:T(8,128)(2,1)S(1)}, bf16[512,1024]{1,0:T(8,128)(2,1)S(1)}) custom-call(bf16[64,8192]{1,0:T(8,128)(2,1)S(1)} %copy-done.1, bf16[1024,8192]{1,0:T(8,128)(2,1)} %w_ref.1), custom_call_target="tpu_custom_call" | custom-call | flops 8589934592 | bytes 150994944 | tf_op jit(solution)/shard_map/pallas_call | solution.py:138
  99.0 0.0 copy-start.2
  99.0 1.1 copy-done.2
  100.0 1.3 copy.48
  101.3 0.0 copy-done.6
  101.3 0.1 constant_dynamic-slice_fusion
  101.4 0.1 copy.47
  101.5 0.0 copy-done.7
  101.5 0.2 select_reduce_fusion
  101.7 2.5 fusion.25
  104.2 5.6 %fusion.36 = (f32[8,512]{1,0:T(8,128)S(1)}, f32[8,512,512]{1,2,0:T(8,128)}) fusion(f32[512,512,8]{1,0,2:T(8,128)S(1)} %fusion.25, pred[512,512]{0,1:T(8,128)(4,1)S(1)} %iota_compare_fusion), kind=kOutput, calls=%fused_computation.46 | output fusion | flops 12583423 | bytes 17055744 | tf_op jit(solution)/shard_map/sub | solution.py:184
  109.8 0.1 multiply_reduce_fusion.1
  109.9 0.3 broadcast_multiply_fusion
  110.2 0.8 copy-done.4
  111.0 4.5 %multiply_reduce_fusion = (f32[512,8]{0,1:T(8,128)S(1)}, bf16[128,8,512]{2,0,1:T(8,128)(2,1)S(1)}) fusion(bf16[512,1024]{0,1:T(8,128)(2,1)S(1)} %copy-done.4, f32[8,512,512]{1,2,0:T(8,128)} %get-tuple-element.15, f32[8,512]{1,0:T(8,128)S(1)} %get-tuple-element.14, bf16[2,512,1024]{2,1,0:T(8,128)(2,1)S(1)} %copy-done, s32[]{:T(128)S(6)} %add.21, ...), kind=kOutput, calls=%fused_computation.22 | convolution fusion | flops 543682560 | bytes 10649608 | tf_op jit(solution)/shard_map/hts,sd->thd/dot_general | solution.py:186
  115.5 3.0 %fusion.17 = bf16[512,1536]{1,0:T(8,128)(2,1)} fusion(bf16[512,1024]{0,1:T(8,128)(2,1)S(1)} %bitcast.80, bf16[192,8,8,128]{3,2,1,0:T(8,128)(2,1)S(1)} %bitcast.74), kind=kOutput, calls=%fused_computation.20 | convolution fusion | flops 1611399168 | bytes 5767168 | tf_op jit(solution)/shard_map/dot_general | solution.py:198
  118.5 0.0 all-reduce.2.cloned.1.call-update
  118.5 0.2 reduce-scatter.2.cloned.1.call-start
  118.7 89.3 %all-reduce.2.cloned.1.call-done = bf16[512,1536]{1,0:T(8,128)(2,1)} async-done(((bf16[512,1536]{1,0:T(8,128)(2,1)}), bf16[512,1536]{1,0:T(8,128)(2,1)}) %all-reduce.2.cloned.1.call-update) | async-done | bytes 1572880 | tf_op jit(solution)/shard_map/psum | solution.py:201
  208.1 0.0 copy-done.3
  208.1 5.0 %convolution_convert_fusion = bf16[1536,1024]{1,0:T(8,128)(2,1)} fusion(bf16[512,1536]{1,0:T(8,128)(2,1)} %all-reduce.2.cloned.1.call-done, bf16[512,1024]{1,0:T(8,128)(2,1)S(1)} %copy-done.3), kind=kOutput, calls=%fused_computation.15 | convolution fusion | flops 1612185600 | bytes 5767168 | tf_op jit(solution)/shard_map/dot_general | solution.py:205
  213.1 0.0 reduce-scatter.2.cloned.1.call-update
  213.1 1.2 copy-done.5
  214.3 6.2 %multiply_convert_fusion = bf16[128,8,512]{2,0,1:T(8,128)(2,1)} fusion(f32[8,512]{1,0:T(8,128)S(1)} %bitcast.81, bf16[512,8,128]{0,2,1:T(8,128)(2,1)S(1)} %bitcast.75, f32[8,512,512]{1,2,0:T(8,128)} %get-tuple-element.15, f32[8,512]{1,0:T(8,128)S(1)} %get-tuple-element.14, bf16[2,512,1024]{2,1,0:T(8,128)(2,1)S(1)} %copy-done, s32[]{:T(128)S(6)} %select_n.16, ...), kind=kOutput, calls=%fused_computation.21 | convolution fusion | flops 1083179008 | bytes 10782208 | tf_op jit(solution)/shard_map/hts,sd->thd/dot_general | solution.py:220
  220.5 2.4 copy.40
  222.9 27.5 %reduce-scatter.2.cloned.1.call-done = bf16[384,1024]{1,0:T(8,128)(2,1)} async-done(((bf16[1536,1024]{1,0:T(8,128)(2,1)}), bf16[384,1024]{1,0:T(8,128)(2,1)}) %reduce-scatter.2.cloned.1.call-update) | async-done | bytes 786448 | tf_op jit(solution)/shard_map/reduce_scatter | solution.py:208
  250.4 2.5 convert.1
  (10 shorter events, 0.0 us)
Async XLA Ops:
  7.2 94.6 %copy-start = (bf16[2,512,1024]{2,1,0:T(8,128)(2,1)S(1)}, bf16[2,512,1024]{2,1,0:T(8,128)(2,1)}, u32[]{:S(2)}) copy-start(bf16[2,512,1024]{2,1,0:T(8,128)(2,1)} %param.7) | copy-start | bytes 6291460
  7.2 200.9 %all-reduce.2.cloned.1.call-start = ((), (), s32[]{:S(2)}) async-start(), calls=%async_computation.1 | async-start | bytes 3145728 | tf_op jit(solution)/shard_map/psum | solution.py:201
  7.4 1.3 copy-start.1
  8.7 92.6 %copy-start.6 = (s32[12,64]{1,0:T(8,128)S(1)}, s32[12,64]{1,0:T(8,128)}, u32[]{:S(2)}) copy-start(s32[12,64]{1,0:T(8,128)} %param.10) | copy-start | bytes 9220
  8.7 92.8 %copy-start.7 = (s32[12,1]{0,1:T(1,128)S(1)}, s32[12,1]{0,1:T(1,128)}, u32[]{:S(2)}) copy-start(s32[12,1]{0,1:T(1,128)} %param.11) | copy-start | bytes 148
  99.0 1.1 copy-start.2
  109.8 1.2 copy-start.4
  115.5 92.6 %copy-start.3 = (bf16[512,1024]{1,0:T(8,128)(2,1)S(1)}, bf16[512,1024]{1,0:T(8,128)(2,1)}, u32[]{:S(2)}) copy-start(bf16[512,1024]{1,0:T(8,128)(2,1)} %copy-done.2) | copy-start | bytes 3145732
  118.5 131.9 %reduce-scatter.2.cloned.1.call-start = ((), (), s32[]{:S(2)}) async-start(), calls=%async_computation.2 | async-start | bytes 3932160 | tf_op jit(solution)/shard_map/reduce_scatter | solution.py:208
  213.1 1.2 copy-start.5
Sparse Core Ops, SparseCore 0:
  118.6 89.4 all-reduce.1
  213.2 37.1 reduce-scatter.1

commit v2 on v1

v2 whole, which is shorter than its diff:
```python
import functools
import math

import jax
import jax.numpy as jnp
from jax import lax
from jax.experimental import pallas as pl
from jax.experimental.pallas import tpu as pltpu
from jax.sharding import PartitionSpec as P

H = 64
HD = 128
KVH = 8
CAP = 3
MESH = pl.DeviceIdType.MESH


def route_table(owner_index, groups, capacity):
    chosen = owner_index[:, 0]
    picked_count = chosen.shape[0]
    matches = (chosen[:, None] == chosen[None, :]).astype(jnp.int32)
    order = jnp.arange(picked_count, dtype=jnp.int32)
    earlier = (order[:, None] > order[None, :]).astype(jnp.int32)
    slot_index = jnp.sum(matches * earlier, axis=1)
    target = chosen * capacity + slot_index
    places = jnp.arange(groups * capacity, dtype=jnp.int32)
    return (places[:, None] == target[None, :]).astype(jnp.float32)


def ring_member(place, n):
    late = place // (n // 2)
    return (1 - late) * (2 * place) + late * (2 * (n - 1 - place) + 1)


def ring_place(index, n):
    odd = index % 2
    return (1 - odd) * (index // 2) + odd * (n - 1 - index // 2)


def slot_of(direction, hop, n):
    if hop == 0:
        return 0
    if hop == n // 2:
        return n - 1
    return 2 * hop - 1 + direction


def block_kernel(
    n, cot_ref, w_ref, q_ref, kv_ref, chooser_ref,
    grad_ref, slab_ref, picked_ref,
    held, wbuf, acc, probs, attended, mine, sums,
    send_sem, recv_sem, sum_send, sum_recv, pick_send, pick_recv, local_sem,
):
    rows, width = cot_ref.shape
    half = width // 2
    last = n // 2
    tokens = n * rows
    heads = q_ref.shape[1] // HD
    lanes = mine.shape[1] // 2
    scale = 1.0 / math.sqrt(HD)
    me = lax.axis_index("tensor")
    place = ring_place(me, n)
    to = (ring_member((place + 1) % n, n), ring_member((place + n - 1) % n, n))

    w_copy = pltpu.make_async_copy(w_ref, wbuf, local_sem.at[0])
    w_copy.start()
    own_copy = pltpu.make_async_copy(cot_ref, held.at[0], local_sem.at[1])
    own_copy.start()

    barrier = pltpu.get_barrier_semaphore()
    for target in to:
        pl.semaphore_signal(barrier, inc=1, device_id={"tensor": target}, device_id_type=MESH)
    pl.semaphore_wait(barrier, 2)

    def remote(source, target, send, recv, direction):
        copy = pltpu.make_async_remote_copy(
            src_ref=source,
            dst_ref=target,
            send_sem=send,
            recv_sem=recv,
            device_id={"tensor": to[direction]},
            device_id_type=MESH,
        )
        copy.start()
        return copy

    def send_part(direction, hop, part):
        columns = pl.ds(part * half, half)
        source = cot_ref if hop == 1 else held.at[slot_of(direction, hop - 1, n)]
        return remote(
            source.at[:, columns],
            held.at[slot_of(direction, hop, n), :, columns],
            send_sem.at[direction, hop - 1, part],
            recv_sem.at[direction, hop - 1, part],
            direction,
        )

    def shard_rows(at):
        return pl.ds(pl.multiple_of(ring_member(at, n) * rows, rows), rows)

    def arrival(direction, hop):
        return (place + (n - hop if direction == 0 else hop)) % n

    def side(direction):
        return pl.ds(direction * lanes, lanes)

    def send_sum(direction, step):
        if step == 1:
            source = mine.at[shard_rows(arrival(direction, 1)), side(direction)]
        else:
            source = sums.at[direction, step - 2]
        return remote(
            source,
            sums.at[direction, step - 1],
            sum_send.at[direction, step - 1],
            sum_recv.at[direction, step - 1],
            direction,
        )

    def send_pick(direction, hop):
        columns = pl.ds(0, 2 * lanes) if hop < last else side(direction)
        return remote(
            picked_ref.at[slot_of(direction, hop - 1, n), :, columns],
            picked_ref.at[slot_of(direction, hop, n), :, columns],
            pick_send.at[direction, hop - 1],
            pick_recv.at[direction, hop - 1],
            direction,
        )

    sent, summed, picks = {}, {}, {}

    def sum_step(step):
        for direction in range(2):
            summed[direction, step].wait_recv()
            term = mine[shard_rows(arrival(direction, step + 1)), side(direction)]
            total = sums[direction, step - 1].astype(jnp.float32) + term.astype(jnp.float32)
            if step < n - 1:
                sums[direction, step - 1] = total.astype(jnp.bfloat16)
                summed[direction, step + 1] = send_sum(direction, step + 1)
            else:
                picked_ref[0, :, side(direction)] = total.astype(jnp.bfloat16)
        if step == n - 1:
            for direction in range(2):
                picks[direction, 1] = send_pick(direction, 1)

    def pick_step(hop):
        for direction in range(2):
            picks[direction, hop].wait_recv()
            if hop < last:
                picks[direction, hop + 1] = send_pick(direction, hop + 1)

    small = [functools.partial(sum_step, step) for step in range(1, n)]
    small += [functools.partial(pick_step, hop) for hop in range(1, last + 1)]

    def advance():
        if small:
            small.pop(0)()

    def parts(direction, hop):
        order = (0, 1) if direction == 0 else (1, 0)
        return order if hop < last else order[:1]

    for turn in range(2):
        for direction in range(2):
            part = parts(direction, 1)[turn]
            sent[direction, 1, part] = send_part(direction, 1, part)

    tile = 128

    def forward(head, carry):
        columns = pl.ds(pl.multiple_of(head * HD, HD), HD)
        for base in range(0, tokens, tile):
            span = base + tile
            score = (
                lax.dot_general(
                    q_ref[base:span, columns],
                    kv_ref[0, :span, :],
                    (((1,), (1,)), ((), ())),
                    preferred_element_type=jnp.float32,
                )
                * scale
            )
            at = lax.broadcasted_iota(jnp.int32, (tile, span), 0) + base
            key_at = lax.broadcasted_iota(jnp.int32, (tile, span), 1)
            score = jnp.where(at >= key_at, score, -jnp.inf)
            weight = jnp.exp(score - jnp.max(score, axis=1, keepdims=True))
            prob = (weight / jnp.sum(weight, axis=1, keepdims=True)).astype(jnp.bfloat16)
            probs[head, base:span, :span] = prob
            if span < tokens:
                probs[head, base:span, span:] = jnp.zeros((tile, tokens - span), jnp.bfloat16)
            attended[base:span, columns] = jnp.dot(
                prob, kv_ref[1, :span, :], preferred_element_type=jnp.float32
            ).astype(jnp.bfloat16)
        return carry

    lax.fori_loop(0, heads, forward, 0)

    def choose(block, carry):
        at = pl.ds(pl.multiple_of(block * tile, tile), tile)
        mine[at, :] = jnp.dot(
            attended[at, :], chooser_ref[...], preferred_element_type=jnp.float32
        ).astype(jnp.bfloat16)
        return carry

    lax.fori_loop(0, tokens // tile, choose, 0)
    for direction in range(2):
        summed[direction, 1] = send_sum(direction, 1)

    own_copy.wait()
    w_copy.wait()
    step_width = 1024
    slab_width = width // n
    my_columns = pl.ds(pl.multiple_of(me * slab_width, slab_width), slab_width)

    def product(first, count):
        acc[...] = jnp.zeros_like(acc)

        def body(k, carry):
            columns = pl.ds(pl.multiple_of(k * step_width, step_width), step_width)
            block = held[first : first + count, :, columns].reshape(count * rows, step_width)
            acc[: count * rows, :] += lax.dot_general(
                block,
                wbuf[:, columns],
                (((1,), (1,)), ((), ())),
                preferred_element_type=jnp.float32,
            )
            return carry

        lax.fori_loop(0, width // step_width, body, 0)

    def backward(slot, at, origin):
        slab_ref[slot] = held[slot, :, my_columns]
        where = shard_rows(origin)

        def body(head, carry):
            columns = pl.ds(pl.multiple_of(head * HD, HD), HD)
            grad = acc[at * rows : (at + 1) * rows, columns].astype(jnp.bfloat16)
            prob_grad = lax.dot_general(
                grad,
                kv_ref[1],
                (((1,), (1,)), ((), ())),
                preferred_element_type=jnp.float32,
            )
            delta = jnp.sum(
                grad.astype(jnp.float32) * attended[where, columns].astype(jnp.float32),
                axis=1,
                keepdims=True,
            )
            score_grad = (probs[head, where, :].astype(jnp.float32) * (prob_grad - delta)).astype(jnp.bfloat16)
            result = jnp.dot(score_grad, kv_ref[0], preferred_element_type=jnp.float32) * scale
            grad_ref[where, columns] = result.astype(jnp.bfloat16)
            return carry

        lax.fori_loop(0, heads, body, 0)

    def event(hop, turn):
        for direction in range(2):
            part = parts(direction, hop)[turn]
            sent[direction, hop, part].wait_recv()
            if hop < last and part in parts(direction, hop + 1):
                sent[direction, hop + 1, part] = send_part(direction, hop + 1, part)

    event(1, 0)
    advance()
    product(0, 1)
    advance()
    event(1, 1)
    advance()
    backward(0, 0, place)
    for hop in range(1, last + 1):
        turns = 2 if hop < last else 1
        if hop > 1:
            event(hop, 0)
            advance()
            if turns == 2:
                event(hop, 1)
                advance()
        product(slot_of(0, hop, n), turns)
        advance()
        for direction in range(turns):
            backward(slot_of(direction, hop, n), direction, arrival(direction, hop))
    while small:
        advance()
    for copies in (sent, summed, picks):
        for copy in copies.values():
            copy.wait_send()


def ring_block(cotangent, out_weight, queries, kv_local, chooser, n):
    rows, width = cotangent.shape
    outs = out_weight.shape[0]
    tokens = n * rows
    lanes = chooser.shape[1] // 2
    vmem = pl.BlockSpec(memory_space=pltpu.VMEM)
    hbm = pl.BlockSpec(memory_space=pl.ANY)
    dma = pltpu.SemaphoreType.DMA
    return pl.pallas_call(
        functools.partial(block_kernel, n),
        out_shape=(
            jax.ShapeDtypeStruct((tokens, outs), jnp.bfloat16),
            jax.ShapeDtypeStruct((n, rows, width // n), jnp.bfloat16),
            jax.ShapeDtypeStruct((n, rows, 2 * lanes), jnp.bfloat16),
        ),
        in_specs=[hbm, hbm, vmem, vmem, vmem],
        out_specs=(vmem, vmem, vmem),
        scratch_shapes=[
            pltpu.VMEM((n, rows, width), jnp.bfloat16),
            pltpu.VMEM((outs, width), jnp.bfloat16),
            pltpu.VMEM((2 * rows, outs), jnp.float32),
            pltpu.VMEM((outs // HD, tokens, tokens), jnp.bfloat16),
            pltpu.VMEM((tokens, outs), jnp.bfloat16),
            pltpu.VMEM((tokens, 2 * lanes), jnp.bfloat16),
            pltpu.VMEM((2, n - 1, rows, lanes), jnp.bfloat16),
            dma((2, n // 2, 2)),
            dma((2, n // 2, 2)),
            dma((2, n - 1)),
            dma((2, n - 1)),
            dma((2, n // 2)),
            dma((2, n // 2)),
            dma((2,)),
        ],
        compiler_params=pltpu.CompilerParams(
            collective_id=0, has_side_effects=True, vmem_limit_bytes=63 * 1024 * 1024
        ),
    )(cotangent, out_weight, queries, kv_local, chooser)


def owner_kernel(m, part_ref, out_ref, inbox, total, core_send, core_recv, far_send, far_recv):
    chips = m // 2
    me = lax.axis_index("dp")
    chip, core = me // 2, me % 2
    partner = chip * 2 + 1 - core
    barrier = pltpu.get_barrier_semaphore()
    peers = [partner] + [((chip + j) % chips) * 2 + core for j in range(1, chips)]
    for peer in peers:
        pl.semaphore_signal(barrier, inc=1, device_id={"dp": peer}, device_id_type=MESH)
    pl.semaphore_wait(barrier, len(peers))
    pieces = CAP
    rows = out_ref.shape[0] // pieces

    copies = []

    def remote(source, target, send, recv, peer):
        copy = pltpu.make_async_remote_copy(
            src_ref=source, dst_ref=target, send_sem=send, recv_sem=recv,
            device_id={"dp": peer}, device_id_type=MESH,
        )
        copy.start()
        copies.append(copy)
        return copy

    near = {}
    for j in list(range(1, chips)) + [0]:
        for piece in range(pieces):
            at = pl.ds(piece * rows, rows)
            owner = ((chip + j) % chips) * 2 + 1 - core
            near[j, piece] = remote(
                part_ref.at[owner, at], inbox.at[0, j, at],
                core_send.at[j, piece], core_recv.at[j, piece], partner,
            )
    far = {}
    for j in range(1, chips):
        owner = ((chip + j) % chips) * 2 + core
        for piece in range(pieces):
            at = pl.ds(piece * rows, rows)
            near[j, piece].wait_recv()
            both = part_ref[owner, at].astype(jnp.float32) + inbox[0, j, at].astype(jnp.float32)
            total[j - 1, at] = both.astype(jnp.bfloat16)
            far[j, piece] = remote(
                total.at[j - 1, at], inbox.at[1, j, at],
                far_send.at[j, piece], far_recv.at[j, piece], owner,
            )
    for piece in range(pieces):
        at = pl.ds(piece * rows, rows)
        near[0, piece].wait_recv()
        out_ref[at] = part_ref[me, at].astype(jnp.float32) + inbox[0, 0, at].astype(jnp.float32)
    for piece in range(pieces):
        at = pl.ds(piece * rows, rows)
        for j in range(1, chips):
            far[j, piece].wait_recv()
            out_ref[at] += inbox[1, j, at].astype(jnp.float32)
    for copy in copies:
        copy.wait_send()


def sum_at_owners(parts):
    owners, rows, columns = parts.shape
    chips = owners // 2
    dma = pltpu.SemaphoreType.DMA
    vmem = pl.BlockSpec(memory_space=pltpu.VMEM)
    return pl.pallas_call(
        functools.partial(owner_kernel, owners),
        out_shape=jax.ShapeDtypeStruct((rows, columns), jnp.float32),
        in_specs=[vmem],
        out_specs=vmem,
        scratch_shapes=[
            pltpu.VMEM((2, chips, rows, columns), jnp.bfloat16),
            pltpu.VMEM((max(chips - 1, 1), rows, columns), jnp.bfloat16),
            dma((chips, CAP)),
            dma((chips, CAP)),
            dma((chips, CAP)),
            dma((chips, CAP)),
        ],
        compiler_params=pltpu.CompilerParams(
            collective_id=1, has_side_effects=True, vmem_limit_bytes=32 * 1024 * 1024
        ),
    )(parts)


def on_device(queries, keys_values, out_weight, cotangent, head_pick, owner_index):
    tensor_size = lax.axis_size("tensor")
    tensor_rank = lax.axis_index("tensor")
    owners = lax.axis_size("dp")
    local_heads = queries.shape[1] // HD
    kv_head = tensor_rank * local_heads // (H // KVH)
    kv_local = lax.dynamic_slice_in_dim(keys_values, kv_head * HD, HD, 2)

    routing = route_table(owner_index, owners, CAP)
    places = routing.shape[0]
    local_pick = lax.dynamic_slice_in_dim(head_pick, tensor_rank * local_heads, local_heads, 1)
    wanted = jnp.sum(routing[:, :, None] * local_pick.astype(jnp.float32)[None], axis=1)
    spread = jnp.repeat(jnp.repeat(wanted.T, HD, axis=0), HD, axis=1)
    row = lax.broadcasted_iota(jnp.int32, spread.shape, 0) % HD
    column = lax.broadcasted_iota(jnp.int32, spread.shape, 1) % HD
    chooser = jnp.where(row == column, spread, 0.0).astype(jnp.bfloat16)

    query_grad, column_slab, picked = ring_block(
        cotangent, out_weight, queries, kv_local, chooser, tensor_size
    )
    tokens = queries.shape[0]
    selected = lax.dot_general(
        picked.reshape(tokens, places * HD),
        column_slab.reshape(tokens, -1),
        (((0,), (0,)), ((), ())),
        preferred_element_type=jnp.float32,
    ).astype(jnp.bfloat16)
    owned = sum_at_owners(selected.reshape(owners, CAP * HD, -1))
    return (query_grad, owned.reshape(CAP, HD, -1))


def solution(mesh):
    placed = (
        P("dp", "tensor"),
        P(None, "dp", None),
        P("tensor", None),
        P(("dp", "tensor"), None),
        P(),
        P(),
    )
    return jax.shard_map(
        on_device,
        mesh=mesh,
        in_specs=placed,
        out_specs=(P("dp", "tensor"), P("dp", None, "tensor")),
        check_vma=False,
    )
```

time: 260 us -> 179 us (0.69)
  waiting for transfers between devices: 117 us -> 0 us
  Pallas kernels: 90.2 us -> 161 us
  matrix products: 21.1 us -> 3.52 us
  between operations: 14.2 us -> 0.75 us
  other arithmetic: 8.69 us -> 4.05 us
    psum x1 -> x0, waiting for transfers between devices: 89.3 us -> none  [on_device(): picked = lax.psum(mine, 'tensor')]
    pallas_call x1 -> x2, Pallas kernels: 90.2 us -> 161 us  [the longest x1 140 us: ring_block(): pl.pallas_call(functools.partial(block_kernel, n), out_shape=(jax.ShapeDt...]
    reduce_scatter x1 -> x0, waiting for transfers between devices: 27.5 us -> none  [on_device(): owned = lax.psum_scatter(selected, 'dp', scatter_dimension=0, tiled=True)]
    dot_general x5 -> x1, matrix products: 21.1 us -> 3.52 us  [on_device(): lax.dot_general(picked.reshape(tokens, places * HD), column_slab.reshape(...]
    sub x1 -> x0, other arithmetic: 5.56 us -> none  [on_device(): weights = jnp.exp(scores - peak)]
    unnamed x18 -> x10, local copies, waits for them, and re-layouts: 6.94 us -> 2.3 us
  transfers between devices with their start and end apart: 2 -> 0, of which waited for: 2 -> 0; matrix products, arithmetic and copies ran while one was open for 3% -> 0% of each run, Pallas kernels for 0% -> 0%
where the time goes in v2:
time: 179 us
  Pallas kernels  161 us (90%)
  local copies, waits for them, and re-layouts  9.3 us (5%)
  other arithmetic  4.05 us (2%)
  matrix products  3.52 us (2%)
    pallas_call x1, Pallas kernels, ring_block(): pl.pallas_call(functools.partial(block_kernel, n), out_shape=(jax.ShapeDt...  140 us
    pallas_call x1, Pallas kernels, sum_at_owners(): pl.pallas_call(functools.partial(owner_kernel, owners), out_shape=jax.Sha...  21.7 us

profile of v2, /device:TPU:0, one launch (start us, length us, event | category | flops | bytes accessed | tf_op | source)
XLA Modules:
  0.0 178.8 jit_solution(13948048238339344459)
XLA Ops:
  0.6 0.0 copy-start
  0.7 0.9 select_reduce_fusion
  1.6 0.7 multiply_add_fusion
  2.3 0.0 copy-done
  2.3 0.1 constant_dynamic-slice_fusion
  2.3 0.1 copy.13
  2.4 0.1 multiply_reduce_fusion
  2.6 0.1 broadcast_bitcast_fusion
  2.7 1.7 constant_dynamic-slice_fusion.1.kv_ref
  4.3 2.1 %broadcast_in_dim.8 = bf16[1024,12,128]{0,2,1:T(8,128)(2,1)} broadcast(bf16[1024,12]{0,1:T(8,128)(2,1)S(1)} %bitcast.19), dimensions={0,1} | broadcast | bytes 3170304 | tf_op jit(solution)/shard_map/broadcast_in_dim | solution.py:422
  6.4 3.2 %copy.12 = bf16[1024,1536]{1,0:T(8,128)(2,1)S(1)} copy(bf16[1024,1536]{0,1:T(8,128)(2,1)} %bitcast.18) | data formatting | bytes 6291456 | tf_op jit(solution)/shard_map/reshape | solution.py:422
  9.6 2.4 %select_convert_fusion.chooser_ref = bf16[1024,1536]{1,0:T(8,128)(2,1)} fusion(bf16[1024,1536]{1,0:T(8,128)(2,1)S(1)} %copy.12, s32[1536]{0:T(1024)S(1)} %get-tuple-element.8, s32[1536]{0:T(1024)S(1)} %get-tuple-element.9, s32[1024]{0:T(1024)S(1)} %get-tuple-element.10, s32[1024]{0:T(1024)S(1)} %get-tuple-element.11, pred[1024]{0:T(1024)(128)(4,1)S(1)} %fusion.8, ...), kind=kLoop, calls=%fused_computation.1 | loop fusion | flops 6291456 | bytes 6314496 | tf_op jit(solution)/shard_map/convert_element_type | solution.py:425
  11.9 139.5 %shard_map.77 = (bf16[512,1024]{1,0:T(8,128)(2,1)}, bf16[8,64,1024]{2,1,0:T(8,128)(2,1)}, bf16[8,64,1536]{2,1,0:T(8,128)(2,1)}) custom-call(bf16[64,8192]{1,0:T(8,128)(2,1)} %cot_ref.1, bf16[1024,8192]{1,0:T(8,128)(2,1)} %w_ref.1, bf16[512,1024]{1,0:T(8,128)(2,1)} %q_ref.1, bf16[2,512,128]{2,1,0:T(8,128)(2,1)} %constant_dynamic-slice_fusion.1.kv_ref, ...), custom_call_target="tpu_custom_call" | custom-call | tf_op jit(solution)/shard_map/pallas_call | solution.py:297
  151.5 3.5 %bitcast_convert_fusion = bf16[1536,1024]{1,0:T(8,128)(2,1)S(1)} fusion(bf16[8,64,1536]{2,1,0:T(8,128)(2,1)} %get-tuple-element.6, bf16[8,64,1024]{2,1,0:T(8,128)(2,1)} %get-tuple-element.7), kind=kOutput, calls=%fused_computation | convolution fusion | flops 1612185600 | bytes 5767168 | tf_op jit(solution)/shard_map/dot_general | solution.py:431
  155.0 0.0 copy-start.1
  155.0 21.7 %shard_map.78 = f32[384,1024]{1,0:T(8,128)S(1)} custom-call(bf16[4,384,1024]{2,1,0:T(8,128)(2,1)S(1)} %bitcast.17), custom_call_target="tpu_custom_call" | custom-call | tf_op jit(solution)/shard_map/pallas_call | solution.py:391
  176.7 0.0 copy-done.1
  176.7 1.0 copy.17
  177.7 1.1 copy.18
  (8 shorter events, 0.0 us)
Async XLA Ops:
  0.6 1.6 copy-start
  155.0 21.7 %copy-start.1 = (bf16[512,1024]{1,0:T(8,128)(2,1)S(1)}, bf16[512,1024]{1,0:T(8,128)(2,1)}, u32[]{:S(2)}) copy-start(bf16[512,1024]{1,0:T(8,128)(2,1)} %get-tuple-element.14) | copy-start | bytes 3145732

commit v3 on v2

--- a/solution.py
+++ b/solution.py
@@ -12,19 +12,11 @@
 HD = 128
 KVH = 8
 CAP = 3
+HD_BITS = 7
+PARTS = 4
+WINDOW = 2
+UNROLL = 4
 MESH = pl.DeviceIdType.MESH
-
-
-def route_table(owner_index, groups, capacity):
-    chosen = owner_index[:, 0]
-    picked_count = chosen.shape[0]
-    matches = (chosen[:, None] == chosen[None, :]).astype(jnp.int32)
-    order = jnp.arange(picked_count, dtype=jnp.int32)
-    earlier = (order[:, None] > order[None, :]).astype(jnp.int32)
-    slot_index = jnp.sum(matches * earlier, axis=1)
-    target = chosen * capacity + slot_index
-    places = jnp.arange(groups * capacity, dtype=jnp.int32)
-    return (places[:, None] == target[None, :]).astype(jnp.float32)
 
 
 def ring_member(place, n):
@@ -46,13 +38,13 @@
 
 
 def block_kernel(
-    n, cot_ref, w_ref, q_ref, kv_ref, chooser_ref,
+    n, cot_ref, w_ref, all_kv_ref, q_ref, pick_ref, owner_ref, owner_row_ref,
     grad_ref, slab_ref, picked_ref,
-    held, wbuf, acc, probs, attended, mine, sums,
+    held, wbuf, kv_ref, chooser_ref, acc, probs, attended, mine, sums,
     send_sem, recv_sem, sum_send, sum_recv, pick_send, pick_recv, local_sem,
 ):
     rows, width = cot_ref.shape
-    half = width // 2
+    piece = width // PARTS
     last = n // 2
     tokens = n * rows
     heads = q_ref.shape[1] // HD
@@ -66,6 +58,11 @@
     w_copy.start()
     own_copy = pltpu.make_async_copy(cot_ref, held.at[0], local_sem.at[1])
     own_copy.start()
+    kv_head = me * heads // (H // KVH)
+    kv_copy = pltpu.make_async_copy(
+        all_kv_ref.at[:, :, pl.ds(pl.multiple_of(kv_head * HD, HD), HD)], kv_ref, local_sem.at[2]
+    )
+    kv_copy.start()
 
     barrier = pltpu.get_barrier_semaphore()
     for target in to:
@@ -85,7 +82,7 @@
         return copy
 
     def send_part(direction, hop, part):
-        columns = pl.ds(part * half, half)
+        columns = pl.ds(part * piece, piece)
         source = cot_ref if hop == 1 else held.at[slot_of(direction, hop - 1, n)]
         return remote(
             source.at[:, columns],
@@ -156,14 +153,45 @@
         if small:
             small.pop(0)()
 
-    def parts(direction, hop):
-        order = (0, 1) if direction == 0 else (1, 0)
-        return order if hop < last else order[:1]
-
-    for turn in range(2):
+    turns = [(hop, turn) for hop in range(1, last) for turn in range(PARTS)]
+    turns += [(last, turn) for turn in range(PARTS // 2)]
+
+    def part_at(direction, turn):
+        return turn if direction == 0 else PARTS - 1 - turn
+
+    def send_turn(number):
+        hop, turn = turns[number]
         for direction in range(2):
-            part = parts(direction, 1)[turn]
-            sent[direction, 1, part] = send_part(direction, 1, part)
+            part = part_at(direction, turn)
+            sent[direction, hop, part] = send_part(direction, hop, part)
+
+    ahead = min(PARTS, len(turns))
+    for number in range(ahead):
+        send_turn(number)
+
+    count = owner_ref.shape[0]
+    chosen = owner_ref[...]
+    order = lax.broadcasted_iota(jnp.int32, (count, count), 0)
+    other = lax.broadcasted_iota(jnp.int32, (count, count), 1)
+    alike = (chosen == owner_row_ref[...]) & (order > other)
+    slot_index = jnp.sum(jnp.where(alike, 1.0, 0.0), axis=1, keepdims=True)
+    goal = chosen.astype(jnp.float32) * CAP + slot_index
+    place_at = lax.broadcasted_iota(jnp.int32, (count, 2 * lanes), 1) >> HD_BITS
+    routed = jnp.where(goal == place_at.astype(jnp.float32), 1.0, 0.0)
+    head_at = lax.broadcasted_iota(jnp.int32, (q_ref.shape[1], H), 0) >> HD_BITS
+    head_of = lax.broadcasted_iota(jnp.int32, (q_ref.shape[1], H), 1)
+    local = jnp.where(head_at + me * heads == head_of, 1.0, 0.0)
+    named = lax.dot_general(
+        local,
+        pick_ref[...].astype(jnp.float32),
+        (((1,), (1,)), ((), ())),
+        preferred_element_type=jnp.float32,
+    )
+    spread = jnp.dot(named, routed, preferred_element_type=jnp.float32)
+    row = lax.broadcasted_iota(jnp.int32, spread.shape, 0) & (HD - 1)
+    column = lax.broadcasted_iota(jnp.int32, spread.shape, 1) & (HD - 1)
+    chooser_ref[...] = jnp.where(row == column, spread, 0.0).astype(jnp.bfloat16)
+    kv_copy.wait()
 
     tile = 128
 
@@ -212,8 +240,9 @@
     slab_width = width // n
     my_columns = pl.ds(pl.multiple_of(me * slab_width, slab_width), slab_width)
 
-    def product(first, count):
-        acc[...] = jnp.zeros_like(acc)
+    def product(first, count, begin, end):
+        if begin == 0:
+            acc[...] = jnp.zeros_like(acc)
 
         def body(k, carry):
             columns = pl.ds(pl.multiple_of(k * step_width, step_width), step_width)
@@ -226,7 +255,8 @@
             )
             return carry
 
-        lax.fori_loop(0, width // step_width, body, 0)
+        steps = width // step_width
+        lax.fori_loop(begin * steps // 2, end * steps // 2, body, 0)
 
     def backward(slot, at, origin):
         slab_ref[slot] = held[slot, :, my_columns]
@@ -251,46 +281,44 @@
             grad_ref[where, columns] = result.astype(jnp.bfloat16)
             return carry
 
-        lax.fori_loop(0, heads, body, 0)
-
-    def event(hop, turn):
+        lax.fori_loop(0, heads, body, 0, unroll=UNROLL)
+
+    work = []
+
+    def queue(first, origins):
+        count = len(origins)
+        work.append(functools.partial(product, first, count, 0, 1))
+        work.append(functools.partial(product, first, count, 1, 2))
+        for at, origin in enumerate(origins):
+            work.append(functools.partial(backward, first + at, at, origin))
+
+    queue(0, [place])
+    for number, (hop, turn) in enumerate(turns):
         for direction in range(2):
-            part = parts(direction, hop)[turn]
-            sent[direction, hop, part].wait_recv()
-            if hop < last and part in parts(direction, hop + 1):
-                sent[direction, hop + 1, part] = send_part(direction, hop + 1, part)
-
-    event(1, 0)
-    advance()
-    product(0, 1)
-    advance()
-    event(1, 1)
-    advance()
-    backward(0, 0, place)
-    for hop in range(1, last + 1):
-        turns = 2 if hop < last else 1
-        if hop > 1:
-            event(hop, 0)
-            advance()
-            if turns == 2:
-                event(hop, 1)
-                advance()
-        product(slot_of(0, hop, n), turns)
+            sent[direction, hop, part_at(direction, turn)].wait_recv()
+        if ahead <= number + WINDOW < len(turns):
+            send_turn(number + WINDOW)
         advance()
-        for direction in range(turns):
-            backward(slot_of(direction, hop, n), direction, arrival(direction, hop))
-    while small:
+        if number + 1 == len(turns):
+            queue(n - 1, [arrival(0, last)])
+        elif turns[number + 1][0] != hop:
+            queue(slot_of(0, hop, n), [arrival(0, hop), arrival(1, hop)])
+        if work:
+            work.pop(0)()
+    while small or work:
         advance()
+        if work:
+            work.pop(0)()
     for copies in (sent, summed, picks):
         for copy in copies.values():
             copy.wait_send()
 
 
-def ring_block(cotangent, out_weight, queries, kv_local, chooser, n):
+def ring_block(cotangent, out_weight, keys_values, queries, head_pick, owner_index, places, n):
     rows, width = cotangent.shape
     outs = out_weight.shape[0]
     tokens = n * rows
-    lanes = chooser.shape[1] // 2
+    lanes = places * HD // 2
     vmem = pl.BlockSpec(memory_space=pltpu.VMEM)
     hbm = pl.BlockSpec(memory_space=pl.ANY)
     dma = pltpu.SemaphoreType.DMA
@@ -301,28 +329,33 @@
             jax.ShapeDtypeStruct((n, rows, width // n), jnp.bfloat16),
             jax.ShapeDtypeStruct((n, rows, 2 * lanes), jnp.bfloat16),
         ),
-        in_specs=[hbm, hbm, vmem, vmem, vmem],
+        in_specs=[hbm, hbm, hbm, vmem, vmem, vmem, vmem],
         out_specs=(vmem, vmem, vmem),
         scratch_shapes=[
             pltpu.VMEM((n, rows, width), jnp.bfloat16),
             pltpu.VMEM((outs, width), jnp.bfloat16),
+            pltpu.VMEM((2, tokens, HD), jnp.bfloat16),
+            pltpu.VMEM((outs, 2 * lanes), jnp.bfloat16),
             pltpu.VMEM((2 * rows, outs), jnp.float32),
             pltpu.VMEM((outs // HD, tokens, tokens), jnp.bfloat16),
             pltpu.VMEM((tokens, outs), jnp.bfloat16),
             pltpu.VMEM((tokens, 2 * lanes), jnp.bfloat16),
             pltpu.VMEM((2, n - 1, rows, lanes), jnp.bfloat16),
-            dma((2, n // 2, 2)),
-            dma((2, n // 2, 2)),
+            dma((2, n // 2, PARTS)),
+            dma((2, n // 2, PARTS)),
             dma((2, n - 1)),
             dma((2, n - 1)),
             dma((2, n // 2)),
             dma((2, n // 2)),
-            dma((2,)),
+            dma((3,)),
         ],
         compiler_params=pltpu.CompilerParams(
             collective_id=0, has_side_effects=True, vmem_limit_bytes=63 * 1024 * 1024
         ),
-    )(cotangent, out_weight, queries, kv_local, chooser)
+    )(
+        cotangent, out_weight, keys_values, queries,
+        head_pick, owner_index, owner_index.reshape(1, -1),
+    )
 
 
 def owner_kernel(m, part_ref, out_ref, inbox, total, core_send, core_recv, far_send, far_recv):
@@ -409,23 +442,10 @@
 
 def on_device(queries, keys_values, out_weight, cotangent, head_pick, owner_index):
     tensor_size = lax.axis_size("tensor")
-    tensor_rank = lax.axis_index("tensor")
     owners = lax.axis_size("dp")
-    local_heads = queries.shape[1] // HD
-    kv_head = tensor_rank * local_heads // (H // KVH)
-    kv_local = lax.dynamic_slice_in_dim(keys_values, kv_head * HD, HD, 2)
-
-    routing = route_table(owner_index, owners, CAP)
-    places = routing.shape[0]
-    local_pick = lax.dynamic_slice_in_dim(head_pick, tensor_rank * local_heads, local_heads, 1)
-    wanted = jnp.sum(routing[:, :, None] * local_pick.astype(jnp.float32)[None], axis=1)
-    spread = jnp.repeat(jnp.repeat(wanted.T, HD, axis=0), HD, axis=1)
-    row = lax.broadcasted_iota(jnp.int32, spread.shape, 0) % HD
-    column = lax.broadcasted_iota(jnp.int32, spread.shape, 1) % HD
-    chooser = jnp.where(row == column, spread, 0.0).astype(jnp.bfloat16)
-
+    places = owners * CAP
     query_grad, column_slab, picked = ring_block(
-        cotangent, out_weight, queries, kv_local, chooser, tensor_size
+        cotangent, out_weight, keys_values, queries, head_pick, owner_index, places, tensor_size
     )
     tokens = queries.shape[0]
     selected = lax.dot_general(

time: 179 us -> 162 us (0.905)
  Pallas kernels: 161 us -> 154 us
  local copies, waits for them, and re-layouts: 9.3 us -> 3.46 us
  other arithmetic: 4.05 us -> 0 us
    pallas_call x1, Pallas kernels: 140 us -> 133 us  [ring_block(): pl.pallas_call(functools.partial(block_kernel, n), out_shape=(jax.ShapeDt...]
    reshape x1 -> x0, local copies, waits for them, and re-layouts: 3.18 us -> none  [on_device(): spread = jnp.repeat(jnp.repeat(wanted.T, HD, axis=0), HD, axis=1)]
    convert_element_type x3 -> x0, other arithmetic: 2.36 us -> none  [the longest x1 2.35 us: on_device(): chooser = jnp.where(row == column, spread, 0.0).astype(jnp.bfloat16)]
    broadcast_in_dim x1 -> x0, local copies, waits for them, and re-layouts: 2.07 us -> none  [on_device(): spread = jnp.repeat(jnp.repeat(wanted.T, HD, axis=0), HD, axis=1)]
where the time goes in v3:
time: 162 us
  Pallas kernels  154 us (95%)
  matrix products  3.52 us (2%)
  local copies, waits for them, and re-layouts  3.46 us (2%)
    pallas_call x1, Pallas kernels, ring_block(): pl.pallas_call(functools.partial(block_kernel, n), out_shape=(jax.ShapeDt...  133 us
    pallas_call x1, Pallas kernels, sum_at_owners(): pl.pallas_call(functools.partial(owner_kernel, owners), out_shape=jax.Sha...  21.6 us
    dot_general x1, matrix products, on_device(): lax.dot_general(picked.reshape(tokens, places * HD), column_slab.reshape(...  3.52 us
    unnamed x5, local copies, waits for them, and re-layouts  3.46 us

profile of v3, /device:TPU:0, one launch (start us, length us, event | category | flops | bytes accessed | tf_op | source)
XLA Modules:
  0.0 161.8 jit_solution(3506059259815333315)
XLA Ops:
  0.6 1.3 copy.8.owner_ref
  2.0 132.5 %shard_map.77 = (bf16[512,1024]{1,0:T(8,128)(2,1)}, bf16[8,64,1024]{2,1,0:T(8,128)(2,1)}, bf16[8,64,1536]{2,1,0:T(8,128)(2,1)}) custom-call(bf16[64,8192]{1,0:T(8,128)(2,1)} %cot_ref.1, bf16[1024,8192]{1,0:T(8,128)(2,1)} %w_ref.1, bf16[2,512,1024]{2,1,0:T(8,128)(2,1)} %all_kv_ref.1, bf16[512,1024]{1,0:T(8,128)(2,1)} %q_ref.1, s32[12,64]{1,0:T(8,128)} %pick_ref.1, ...), custom_call_target="tpu_custom_call" | custom-call | tf_op jit(solution)/shard_map/pallas_call | solution.py:325
  134.5 3.5 %bitcast_convert_fusion = bf16[1536,1024]{1,0:T(8,128)(2,1)S(1)} fusion(bf16[8,64,1536]{2,1,0:T(8,128)(2,1)} %get-tuple-element.6, bf16[8,64,1024]{2,1,0:T(8,128)(2,1)} %get-tuple-element.7), kind=kOutput, calls=%fused_computation | convolution fusion | flops 1612185600 | bytes 5767168 | tf_op jit(solution)/shard_map/dot_general | solution.py:451
  138.0 0.0 copy-start
  138.1 21.6 %shard_map.78 = f32[384,1024]{1,0:T(8,128)S(1)} custom-call(bf16[4,384,1024]{2,1,0:T(8,128)(2,1)S(1)} %bitcast.8), custom_call_target="tpu_custom_call" | custom-call | tf_op jit(solution)/shard_map/pallas_call | solution.py:424
  159.7 0.0 copy-done
  159.7 1.0 copy.11
  160.7 1.1 copy.12
Async XLA Ops:
  138.0 21.7 %copy-start = (bf16[512,1024]{1,0:T(8,128)(2,1)S(1)}, bf16[512,1024]{1,0:T(8,128)(2,1)}, u32[]{:S(2)}) copy-start(bf16[512,1024]{1,0:T(8,128)(2,1)} %get-tuple-element.10) | copy-start | bytes 3145732
